TPU v7x, 512 devices: a whole 4x8x8 slice. The times are simulated.
512 devices in a mesh: fsdp: 64 (over x, z, y_hi), dp: 8 (over y_lo, core).
Axes of the slice: x: 4, y: 8 (y_hi: 2, y_lo: 4; y = y_hi * 4 + y_lo), z: 8, core: 2. Of those that a mesh axis runs over, the one named last changes fastest.
Arguments:
- tokens: bfloat16 [65536, 8192], P(('fsdp', 'dp')), may hold values from -6 to 6
- token_adapter_index: int32 [65536, 1], P(('fsdp', 'dp')), may hold values from 0 to 63; in each aligned block of 128 rows (0 to 127, 128 to 255, ...) at most 3 rows name the same one
- adapter_storage_index: int32 [64], replicated, may hold values from 0 to 63, each once
- frozen_value_weight: bfloat16 [8192, 512], P(('fsdp', 'dp')), may hold values from -0.0625 to 0.0625
- frozen_value_bias: bfloat16 [512], replicated, may hold values from -3 to 3
- adapter_down_weight: bfloat16 [64, 8192, 64], P('fsdp'), may hold values from -0.0625 to 0.0625
- adapter_up_weight: bfloat16 [64, 64, 512], P('fsdp'), may hold values from -0.75 to 0.75
- cotangent: bfloat16 [65536, 512], P(('fsdp', 'dp')), may hold values from -0.1875 to 0.1875
Outputs:
- values: bfloat16 [65536, 512], P(('fsdp', 'dp'))
- grad_down: float32 [64, 8192, 64], P('fsdp', 'dp')
- grad_up: float32 [64, 64, 512], P('fsdp', None, 'dp')
Inputs may be any that keep to these rules, and one draw needn't show every extreme that they name: `token_adapter_index`: within the 128 rows of one device no adapter is named by more than 3 rows. `adapter_storage_index`: each storage index appears once.
All inputs are finite; a program needn't handle non-finite values.
Results may differ from a plain program's by a relative error of at most 0.0048.
Values may be sent and summed in bfloat16 or wider, within the bound.
No kernel may reach another device: no remote copies, remote signals or barrier semaphores. Data moves between devices by JAX's collectives and lax.ppermute only.
A program may use at most 64 MiB of HBM per device.

v0:
```python
import jax
import jax.numpy as jnp
from jax import lax
from jax.sharding import PartitionSpec as P


def body(
    tokens,
    token_adapter_index,
    adapter_storage_index,
    frozen_value_weight,
    frozen_value_bias,
    adapter_down_weight,
    adapter_up_weight,
    cotangent,
):
    token_count, model_width = tokens.shape
    value_width = frozen_value_weight.shape[1]
    fsdp_size = lax.axis_size("fsdp")
    slots_total = adapter_storage_index.shape[0]
    capacity = max(2, (3 * token_count + 2 * fsdp_size - 1) // (2 * fsdp_size))
    base_value = jnp.dot(
        tokens,
        lax.all_gather(frozen_value_weight, ("fsdp", "dp"), axis=0, tiled=True),
        preferred_element_type=jnp.float32,
    )
    base_value = base_value + frozen_value_bias.astype(jnp.float32)
    owner_index = jnp.take(adapter_storage_index, token_adapter_index[:, 0])
    onehot = (owner_index[:, None] == jnp.arange(slots_total)[None, :]).astype(jnp.int32)
    place_in_slot = jnp.sum((jnp.cumsum(onehot, 0) - onehot) * onehot, 1)
    target_row = owner_index * capacity + place_in_slot
    dispatch = (jnp.arange(slots_total * capacity)[:, None] == target_row[None, :]).astype(
        jnp.bfloat16
    )
    sent_rows = jnp.dot(dispatch, tokens, preferred_element_type=jnp.float32).astype(jnp.bfloat16)
    sent_rows = sent_rows.reshape(slots_total, capacity, model_width)
    sent_cot = jnp.dot(dispatch, cotangent, preferred_element_type=jnp.float32).astype(jnp.bfloat16)
    sent_cot = sent_cot.reshape(slots_total, capacity, value_width)
    arrived = lax.all_to_all(sent_rows, "fsdp", split_axis=0, concat_axis=0, tiled=True)
    arrived_rows = arrived.reshape(-1, model_width)
    down_projection = adapter_down_weight[0]
    up_projection = adapter_up_weight[0]
    rank_activation = jnp.dot(
        arrived_rows, down_projection, preferred_element_type=jnp.float32
    ).astype(jnp.bfloat16)
    adapter_delta = jnp.dot(
        rank_activation, up_projection, preferred_element_type=jnp.float32
    ).astype(jnp.bfloat16)
    returned = lax.all_to_all(
        adapter_delta.reshape(fsdp_size, capacity, value_width),
        "fsdp",
        split_axis=0,
        concat_axis=0,
        tiled=True,
    )
    returned = returned.reshape(-1, value_width)
    placed = jnp.einsum("st,sk->tk", dispatch, returned, preferred_element_type=jnp.float32)
    values = (base_value + placed).astype(jnp.bfloat16)
    arrived_cot = lax.all_to_all(sent_cot, "fsdp", split_axis=0, concat_axis=0, tiled=True)
    cotangent_rows = arrived_cot.reshape(-1, value_width)
    rank_cotangent = lax.dot_general(
        cotangent_rows, up_projection, (((1,), (1,)), ((), ())), preferred_element_type=jnp.float32
    ).astype(jnp.bfloat16)
    grad_down = lax.dot_general(
        arrived_rows, rank_cotangent, (((0,), (0,)), ((), ())), preferred_element_type=jnp.float32
    )
    grad_up = lax.dot_general(
        rank_activation,
        cotangent_rows,
        (((0,), (0,)), ((), ())),
        preferred_element_type=jnp.float32,
    )
    summed_down, summed_up = (
        lax.psum_scatter(grad_down, "dp", scatter_dimension=0, tiled=True),
        lax.psum_scatter(grad_up, "dp", scatter_dimension=1, tiled=True),
    )
    return (values, summed_down[None], summed_up[None])


def solution(mesh):
    return jax.shard_map(
        body,
        mesh=mesh,
        in_specs=(
            P(("fsdp", "dp"), None),
            P(("fsdp", "dp"), None),
            P(),
            P(("fsdp", "dp"), None),
            P(),
            P("fsdp", None, None),
            P("fsdp", None, None),
            P(("fsdp", "dp"), None),
        ),
        out_specs=(P(("fsdp", "dp"), None), P("fsdp", "dp", None), P("fsdp", None, "dp")),
        check_vma=False,
    )
```

profile of v0, /device:TPU:1, one launch (start us, length us, event | category | flops | bytes accessed | tf_op | source)
XLA Modules:
  0.0 325.9 jit_solution(2407330163752891406)
XLA Ops:
  8.0 0.8 fusion.13
  8.8 1.6 gather_fusion
  10.4 0.7 fusion.12
  11.5 0.7 fusion.11
  12.2 1.1 convolution_convert_fusion.2
  13.3 0.8 reshape.45
  14.1 19.6 %all-to-all-start.2 = ((bf16[64,3,512]{2,1,0:T(4,128)(2,1)}), bf16[64,3,512]{2,1,0:T(4,128)(2,1)S(1)}, u32[]{:S(2)}, u32[]{:S(2)}) async-start(bf16[64,3,512]{2,1,0:T(4,128)(2,1)} %reshape.45), calls=%async_computation.2 | async-start | bytes 524288 | tf_op jit(solution)/shard_map/all_to_all | solution.py:59
  33.7 2.6 convolution_convert_fusion
  36.3 7.1 %reshape.41 = bf16[64,3,8192]{2,1,0:T(4,128)(2,1)} reshape(bf16[192,8192]{1,0:T(8,128)(2,1)} %convolution_convert_fusion) | data formatting | bytes 6291456 | tf_op jit(solution)/shard_map/reshape | solution.py:36
  43.4 4.0 %all-to-all-done.2 = bf16[64,3,512]{2,1,0:T(4,128)(2,1)S(1)} async-done(((bf16[64,3,512]{2,1,0:T(4,128)(2,1)}), bf16[64,3,512]{2,1,0:T(4,128)(2,1)S(1)}, u32[]{:S(2)}, u32[]{:S(2)}) %all-to-all-start.2) | async-done | bytes 196640 | tf_op jit(solution)/shard_map/all_to_all | solution.py:59
  47.4 10.9 %all-to-all-start = ((bf16[64,3,8192]{2,1,0:T(4,128)(2,1)}), bf16[64,3,8192]{2,1,0:T(4,128)(2,1)}, u32[]{:S(2)}, u32[]{:S(2)}) async-start(bf16[64,3,8192]{2,1,0:T(4,128)(2,1)} %reshape.41), calls=%async_computation | async-start | bytes 8388608 | tf_op jit(solution)/shard_map/all_to_all | solution.py:39
  58.5 94.7 %all-to-all-done = bf16[64,3,8192]{2,1,0:T(4,128)(2,1)} async-done(((bf16[64,3,8192]{2,1,0:T(4,128)(2,1)}), bf16[64,3,8192]{2,1,0:T(4,128)(2,1)}, u32[]{:S(2)}, u32[]{:S(2)}) %all-to-all-start) | async-done | bytes 3145760 | tf_op jit(solution)/shard_map/all_to_all | solution.py:39
  153.1 7.5 %reshape.42 = bf16[192,8192]{1,0:T(8,128)(2,1)} reshape(bf16[64,3,8192]{2,1,0:T(4,128)(2,1)} %all-to-all-done) | data formatting | bytes 6291456 | tf_op jit(solution)/shard_map/reshape | solution.py:40
  160.6 3.0 convolution_convert_fusion.4
  163.6 1.0 convolution_bitcast_fusion
  164.7 0.5 all-gather.2.cloned.1.call-update
  165.3 4.2 %fusion.1 = f32[8192,64]{0,1:T(8,128)} fusion(bf16[192,8192]{1,0:T(8,128)(2,1)} %reshape.42, bf16[192,512]{1,0:T(8,128)(2,1)S(1)} %reshape.46, bf16[1,64,512]{2,1,0:T(8,128)(2,1)S(1)} %copy-done.2), kind=kOutput, calls=%fused_computation.10 | convolution fusion | flops 213921792 | bytes 5505024 | tf_op jit(solution)/shard_map/dot_general | solution.py:64
  169.8 0.8 reshape.43
  170.7 13.7 %all-to-all-start.1 = ((bf16[64,3,512]{2,1,0:T(4,128)(2,1)}), bf16[64,3,512]{2,1,0:T(4,128)(2,1)S(1)}, u32[]{:S(2)}, u32[]{:S(2)}) async-start(bf16[64,3,512]{2,1,0:T(4,128)(2,1)} %reshape.43), calls=%async_computation.1 | async-start | bytes 524288 | tf_op jit(solution)/shard_map/all_to_all | solution.py:49
  184.4 31.2 %reduce-scatter.7.cloned.1.call-done = f32[64,64]{1,0:T(8,128)} async-done(((f32[512,64]{1,0:T(8,128)}), f32[64,64]{1,0:T(8,128)}) %reduce-scatter.7.cloned.1.call-update) | async-done | bytes 16400
  215.6 1.5 copy.12
  217.2 95.7 %all-gather.2.cloned.1.call-done = bf16[8192,512]{1,0:T(8,128)(2,1)} async-done(((bf16[16,512]{1,0:T(8,128)(2,1)}), bf16[8192,512]{1,0:T(8,128)(2,1)}) %all-gather.2.cloned.1.call-update) | async-done | bytes 8388624 | tf_op jit(solution)/shard_map/all_gather | solution.py:24
  312.9 4.6 %convolution_add_fusion.1 = f32[128,512]{1,0:T(8,128)S(1)} fusion(bf16[128,8192]{1,0:T(8,128)(2,1)S(1)} %copy-done, bf16[8192,512]{1,0:T(8,128)(2,1)} %all-gather.2.cloned.1.call-done, f32[512]{0:T(512)S(1)} %convert_element_type.25), kind=kOutput, calls=%fused_computation.6 | convolution fusion | flops 1073807360 | bytes 10749952 | tf_op jit(solution)/shard_map/dot_general | solution.py:22
  317.6 0.9 fusion
  (23 shorter events, 1.2 us)
Async XLA Ops:
  8.0 25.7 %copy-start = (bf16[128,8192]{1,0:T(8,128)(2,1)S(1)}, bf16[128,8192]{1,0:T(8,128)(2,1)}, u32[]{:S(2)}) copy-start(bf16[128,8192]{1,0:T(8,128)(2,1)} %param.8) | copy-start | bytes 6291460
  14.1 33.3 %all-to-all-start.2 = ((bf16[64,3,512]{2,1,0:T(4,128)(2,1)}), bf16[64,3,512]{2,1,0:T(4,128)(2,1)S(1)}, u32[]{:S(2)}, u32[]{:S(2)}) async-start(bf16[64,3,512]{2,1,0:T(4,128)(2,1)} %reshape.45), calls=%async_computation.2 | async-start | bytes 524288 | tf_op jit(solution)/shard_map/all_to_all | solution.py:59
  47.4 105.8 %all-to-all-start = ((bf16[64,3,8192]{2,1,0:T(4,128)(2,1)}), bf16[64,3,8192]{2,1,0:T(4,128)(2,1)}, u32[]{:S(2)}, u32[]{:S(2)}) async-start(bf16[64,3,8192]{2,1,0:T(4,128)(2,1)} %reshape.41), calls=%async_computation | async-start | bytes 8388608 | tf_op jit(solution)/shard_map/all_to_all | solution.py:39
  58.2 157.4 %reduce-scatter.7.cloned.1.call-start = ((), (), s32[]{:S(2)}) async-start(), calls=%async_computation.7 | async-start | bytes 294912
  58.5 102.1 %copy-start.1 = (bf16[1,8192,64]{1,2,0:T(8,128)(2,1)S(1)}, bf16[1,8192,64]{1,2,0:T(8,128)(2,1)}, u32[]{:S(2)}) copy-start(bf16[1,8192,64]{1,2,0:T(8,128)(2,1)} %param.13) | copy-start | bytes 3145732
  160.6 4.7 %copy-start.2 = (bf16[1,64,512]{2,1,0:T(8,128)(2,1)S(1)}, bf16[1,64,512]{2,1,0:T(8,128)(2,1)}, u32[]{:S(2)}) copy-start(bf16[1,64,512]{2,1,0:T(8,128)(2,1)} %param.14) | copy-start | bytes 196612
  164.6 148.3 %all-gather.2.cloned.1.call-start = ((), (), s32[]{:S(2)}) async-start(), calls=%async_computation.5 | async-start | bytes 8404992 | tf_op jit(solution)/shard_map/all_gather | solution.py:24
  165.2 19.1 %copy-start.3 = (bf16[512]{0:T(512)(128)(2,1)S(1)}, bf16[512]{0:T(512)(128)(2,1)}, u32[]{:S(2)}) copy-start(bf16[512]{0:T(512)(128)(2,1)} %param.12) | copy-start | bytes 3076
  165.2 153.2 %reduce-scatter.5.cloned.1.call-start = ((), (), s32[]{:S(2)}) async-start(), calls=%async_computation.6 | async-start | bytes 2359296 | tf_op jit(solution)/shard_map/reduce_scatter | solution.py:74
  170.7 46.4 %all-to-all-start.1 = ((bf16[64,3,512]{2,1,0:T(4,128)(2,1)}), bf16[64,3,512]{2,1,0:T(4,128)(2,1)S(1)}, u32[]{:S(2)}, u32[]{:S(2)}) async-start(bf16[64,3,512]{2,1,0:T(4,128)(2,1)} %reshape.43), calls=%async_computation.1 | async-start | bytes 524288 | tf_op jit(solution)/shard_map/all_to_all | solution.py:49
Sparse Core Ops, SparseCore 0:
  164.8 50.7 reduce-scatter.6
  219.0 43.4 reduce-scatter.4
Sparse Core Ops, SparseCore 1:
  169.6 143.3 all-gather.1
where the time goes:
time: 327 us; the launch traced here: 326 us
  waiting for transfers between devices  226 us (69%)
  starting transfers between devices  44.3 us (14%)
  local copies, waits for them, and re-layouts  19.6 us (6%)
  matrix products  17.7 us (5%)
  between operations  15.6 us (5%)
    all_gather x1, waiting for transfers between devices, body(): lax.all_gather(frozen_value_weight, ('fsdp', 'dp'), axis=0, tiled=True)  95.7 us
    all_to_all x1, waiting for transfers between devices, body(): lax.all_to_all(sent_rows, 'fsdp', split_axis=0, concat_axis=0, tiled=True)  94.7 us
    unnamed x4, waiting for transfers between devices  31.8 us
    all_to_all x1, starting transfers between devices, body(): lax.all_to_all(sent_cot, 'fsdp', split_axis=0, concat_axis=0, tiled=True)  19.6 us
    all_to_all x1, starting transfers between devices, body(): lax.all_to_all(adapter_delta.reshape(fsdp_size, capacity, value_width), '...  13.7 us
    all_to_all x1, starting transfers between devices, body(): lax.all_to_all(sent_rows, 'fsdp', split_axis=0, concat_axis=0, tiled=True)  10.9 us
    reshape x1, local copies, waits for them, and re-layouts, body(): arrived_rows = arrived.reshape(-1, model_width)  7.46 us
    reshape x1, local copies, waits for them, and re-layouts, body(): sent_rows = sent_rows.reshape(slots_total, capacity, model_width)  7.05 us
  transfers between devices with their start and end apart: 6, of which 4 were waited for; matrix products, arithmetic and copies ran while one was open for 7% of the time, Pallas kernels for 0%

commit v1 on v0

--- a/solution.py
+++ b/solution.py
@@ -1,7 +1,18 @@
+import functools
 import jax
 import jax.numpy as jnp
 from jax import lax
 from jax.sharding import PartitionSpec as P
+
+
+def do_classes(field_in, dev_axis, dim_k):
+    arr_next = jnp.concatenate(
+        lax.all_to_all(jnp.stack(lax.psum(1, dev_axis) * [field_in], 0), dev_axis, 0, 0), axis=dim_k
+    )
+    return arr_next
+
+
+_spread_outputs = functools.partial(do_classes, dev_axis=("fsdp", "dp"), dim_k=0)
 
 
 def body(
@@ -20,9 +31,7 @@
     slots_total = adapter_storage_index.shape[0]
     capacity = max(2, (3 * token_count + 2 * fsdp_size - 1) // (2 * fsdp_size))
     base_value = jnp.dot(
-        tokens,
-        lax.all_gather(frozen_value_weight, ("fsdp", "dp"), axis=0, tiled=True),
-        preferred_element_type=jnp.float32,
+        tokens, _spread_outputs(frozen_value_weight), preferred_element_type=jnp.float32
     )
     base_value = base_value + frozen_value_bias.astype(jnp.float32)
     owner_index = jnp.take(adapter_storage_index, token_adapter_index[:, 0])

time: 327 us -> 436 us (1.33)
  waiting for transfers between devices: 226 us -> 300 us
  blocking collectives: 0 us -> 25.4 us
  starting transfers between devices: 44.3 us -> 53.6 us
    all_to_all x1, waiting for transfers between devices: 0.01 us -> 160 us  [do_classes(): lax.all_to_all(jnp.stack(lax.psum(1, dev_axis) * [field_in], 0), dev_axis...]
    all_gather x1 -> x0, waiting for transfers between devices: 95.7 us -> none  [body(): lax.all_gather(frozen_value_weight, ('fsdp', 'dp'), axis=0, tiled=True)]
    all_to_all x0 -> x1, blocking collectives: none -> 25.4 us  [body(): lax.all_to_all(adapter_delta.reshape(fsdp_size, capacity, value_width), '...]
    all_to_all x1, starting transfers between devices: 13.7 us -> 23.4 us  [do_classes(): lax.all_to_all(jnp.stack(lax.psum(1, dev_axis) * [field_in], 0), dev_axis...]
    all_to_all x1, starting transfers between devices: 19.6 us -> 10.1 us  [body(): lax.all_to_all(sent_cot, 'fsdp', split_axis=0, concat_axis=0, tiled=True)]
    all_to_all x1, starting transfers between devices: 10.9 us -> 20 us  [body(): lax.all_to_all(sent_rows, 'fsdp', split_axis=0, concat_axis=0, tiled=True)]
    unnamed x4 -> x3, waiting for transfers between devices: 31.8 us -> 40.7 us
  transfers between devices with their start and end apart: 6 -> 5, of which waited for: 4 -> 4; matrix products, arithmetic and copies ran while one was open for 7% -> 6% of each run, Pallas kernels for 0% -> 0%
where the time goes in v1:
time: 436 us
  waiting for transfers between devices  300 us (69%)
  starting transfers between devices  53.6 us (12%)
  blocking collectives  25.4 us (6%)
  local copies, waits for them, and re-layouts  23.2 us (5%)
  matrix products  16.8 us (4%)
  between operations  14.2 us (3%)
    all_to_all x1, waiting for transfers between devices, do_classes(): lax.all_to_all(jnp.stack(lax.psum(1, dev_axis) * [field_in], 0), dev_axis...  160 us
    all_to_all x1, waiting for transfers between devices, body(): lax.all_to_all(sent_rows, 'fsdp', split_axis=0, concat_axis=0, tiled=True)  96.4 us
    unnamed x3, waiting for transfers between devices  40.7 us
    all_to_all x1, blocking collectives, body(): lax.all_to_all(adapter_delta.reshape(fsdp_size, capacity, value_width), '...  25.4 us
    all_to_all x1, starting transfers between devices, do_classes(): lax.all_to_all(jnp.stack(lax.psum(1, dev_axis) * [field_in], 0), dev_axis...  23.4 us
    all_to_all x1, starting transfers between devices, body(): lax.all_to_all(sent_rows, 'fsdp', split_axis=0, concat_axis=0, tiled=True)  20 us
    all_to_all x1, starting transfers between devices, body(): lax.all_to_all(sent_cot, 'fsdp', split_axis=0, concat_axis=0, tiled=True)  10.1 us
  transfers between devices with their start and end apart: 5, of which 4 were waited for; matrix products, arithmetic and copies ran while one was open for 6% of the time, Pallas kernels for 0%

profile of v1, /device:TPU:1, one launch (start us, length us, event | category | flops | bytes accessed | tf_op | source)
XLA Modules:
  0.0 435.5 jit_solution(13767479986867056603)
XLA Ops:
  7.2 0.8 fusion.13
  8.0 1.6 gather_fusion
  9.6 0.7 fusion.12
  10.7 0.7 fusion.11
  11.4 2.6 convolution_convert_fusion
  14.0 7.1 %reshape.47 = bf16[64,3,8192]{2,1,0:T(4,128)(2,1)} reshape(bf16[192,8192]{1,0:T(8,128)(2,1)} %convolution_convert_fusion) | data formatting | bytes 6291456 | tf_op jit(solution)/shard_map/reshape | solution.py:45
  21.0 20.0 %all-to-all-start.1 = ((bf16[64,3,8192]{2,1,0:T(4,128)(2,1)}), bf16[64,3,8192]{2,1,0:T(4,128)(2,1)}, u32[]{:S(2)}, u32[]{:S(2)}) async-start(bf16[64,3,8192]{2,1,0:T(4,128)(2,1)} %reshape.47), calls=%async_computation.1 | async-start | bytes 8388608 | tf_op jit(solution)/shard_map/all_to_all | solution.py:48
  41.2 0.8 reshape.51
  42.1 96.4 %all-to-all-done.1 = bf16[64,3,8192]{2,1,0:T(4,128)(2,1)} async-done(((bf16[64,3,8192]{2,1,0:T(4,128)(2,1)}), bf16[64,3,8192]{2,1,0:T(4,128)(2,1)}, u32[]{:S(2)}, u32[]{:S(2)}) %all-to-all-start.1) | async-done | bytes 3145760 | tf_op jit(solution)/shard_map/all_to_all | solution.py:48
  138.4 10.1 %all-to-all-start.3 = ((bf16[64,3,512]{2,1,0:T(4,128)(2,1)}), bf16[64,3,512]{2,1,0:T(4,128)(2,1)S(1)}, u32[]{:S(2)}, u32[]{:S(2)}) async-start(bf16[64,3,512]{2,1,0:T(4,128)(2,1)} %reshape.51), calls=%async_computation.3 | async-start | bytes 524288 | tf_op jit(solution)/shard_map/all_to_all | solution.py:68
  148.5 7.5 %reshape.48 = bf16[192,8192]{1,0:T(8,128)(2,1)} reshape(bf16[64,3,8192]{2,1,0:T(4,128)(2,1)} %all-to-all-done.1) | data formatting | bytes 6291456 | tf_op jit(solution)/shard_map/reshape | solution.py:49
  156.1 3.0 convolution_convert_fusion.4
  159.1 0.2 convolution_convert_fusion.1
  159.5 2.7 all-to-all-done.3
  162.2 25.4 %all_to_all.20 = bf16[64,3,512]{2,1,0:T(4,128)(2,1)S(1)} all-to-all(bf16[64,3,512]{2,1,0:T(4,128)(2,1)S(1)} %reshape.49), channel_id=1, replica_groups=mesh['fsdp'=64,'dp'=8] {'fsdp'}, dimensions={0} | all-to-all | bytes 393216 | tf_op jit(solution)/shard_map/all_to_all | solution.py:58
  187.5 4.3 stack.2
  191.8 23.4 %all-to-all-start = ((bf16[512,16,512]{2,1,0:T(8,128)(2,1)}), bf16[512,16,512]{2,1,0:T(8,128)(2,1)}, u32[]{:S(2)}, u32[]{:S(2)}) async-start(bf16[512,16,512]{2,1,0:T(8,128)(2,1)} %stack.2), calls=%async_computation | async-start | bytes 16777216 | tf_op jit(solution)/shard_map/all_to_all | solution.py:10
  215.5 1.0 convolution_bitcast_fusion
  216.6 4.2 fusion.1
  220.8 40.7 %reduce-scatter.7.cloned.1.call-done = f32[64,64]{1,0:T(8,128)} async-done(((f32[512,64]{1,0:T(8,128)}), f32[64,64]{1,0:T(8,128)}) %reduce-scatter.7.cloned.1.call-update) | async-done | bytes 16400
  261.4 1.5 copy.12
  263.1 160.1 %all-to-all-done = bf16[512,16,512]{2,1,0:T(8,128)(2,1)} async-done(((bf16[512,16,512]{2,1,0:T(8,128)(2,1)}), bf16[512,16,512]{2,1,0:T(8,128)(2,1)}, u32[]{:S(2)}, u32[]{:S(2)}) %all-to-all-start) | async-done | bytes 8388640 | tf_op jit(solution)/shard_map/all_to_all | solution.py:10
  423.2 4.6 %convolution_add_fusion.1 = f32[128,512]{1,0:T(8,128)S(1)} fusion(bf16[128,8192]{1,0:T(8,128)(2,1)S(1)} %copy-done, bf16[8192,512]{1,0:T(8,128)(2,1)} %bitcast, f32[512]{0:T(512)S(1)} %convert_element_type.25), kind=kOutput, calls=%fused_computation.6 | convolution fusion | flops 1073807360 | bytes 10749952 | tf_op jit(solution)/shard_map/dot_general | solution.py:33
  427.8 0.9 fusion
  (26 shorter events, 1.2 us)
Async XLA Ops:
  7.2 4.2 copy-start
  21.0 20.0 %copy-start.3 = (bf16[128,512]{1,0:T(8,128)(2,1)S(1)}, bf16[128,512]{1,0:T(8,128)(2,1)}, u32[]{:S(2)}) copy-start(bf16[128,512]{1,0:T(8,128)(2,1)} %param.15) | copy-start | bytes 393220
  21.0 117.4 %all-to-all-start.1 = ((bf16[64,3,8192]{2,1,0:T(4,128)(2,1)}), bf16[64,3,8192]{2,1,0:T(4,128)(2,1)}, u32[]{:S(2)}, u32[]{:S(2)}) async-start(bf16[64,3,8192]{2,1,0:T(4,128)(2,1)} %reshape.47), calls=%async_computation.1 | async-start | bytes 8388608 | tf_op jit(solution)/shard_map/all_to_all | solution.py:48
  138.4 23.7 %all-to-all-start.3 = ((bf16[64,3,512]{2,1,0:T(4,128)(2,1)}), bf16[64,3,512]{2,1,0:T(4,128)(2,1)S(1)}, u32[]{:S(2)}, u32[]{:S(2)}) async-start(bf16[64,3,512]{2,1,0:T(4,128)(2,1)} %reshape.51), calls=%async_computation.3 | async-start | bytes 524288 | tf_op jit(solution)/shard_map/all_to_all | solution.py:68
  148.5 7.6 %copy-start.1 = (bf16[1,8192,64]{1,2,0:T(8,128)(2,1)S(1)}, bf16[1,8192,64]{1,2,0:T(8,128)(2,1)}, u32[]{:S(2)}) copy-start(bf16[1,8192,64]{1,2,0:T(8,128)(2,1)} %param.13) | copy-start | bytes 3145732
  156.1 3.1 copy-start.2
  156.1 31.4 %copy-start.4 = (bf16[16,512]{1,0:T(8,128)(2,1)S(1)}, bf16[16,512]{1,0:T(8,128)(2,1)}, u32[]{:S(2)}) copy-start(bf16[16,512]{1,0:T(8,128)(2,1)} %param.11) | copy-start | bytes 49156
  191.8 231.3 %all-to-all-start = ((bf16[512,16,512]{2,1,0:T(8,128)(2,1)}), bf16[512,16,512]{2,1,0:T(8,128)(2,1)}, u32[]{:S(2)}, u32[]{:S(2)}) async-start(bf16[512,16,512]{2,1,0:T(8,128)(2,1)} %stack.2), calls=%async_computation | async-start | bytes 16777216 | tf_op jit(solution)/shard_map/all_to_all | solution.py:10
  215.3 46.2 %reduce-scatter.7.cloned.1.call-start = ((), (), s32[]{:S(2)}) async-start(), calls=%async_computation.7 | async-start | bytes 294912
  216.5 4.3 copy-start.5
  216.5 212.2 %reduce-scatter.5.cloned.1.call-start = ((), (), s32[]{:S(2)}) async-start(), calls=%async_computation.6 | async-start | bytes 2359296 | tf_op jit(solution)/shard_map/reduce_scatter | solution.py:83
Sparse Core Ops, SparseCore 0:
  218.9 42.5 reduce-scatter.6
  264.8 100.5 reduce-scatter.4
